TPU v7x, 128 devices: a whole 4x4x4 slice. The times are simulated.
128 devices in a mesh: occ: 8 (over y, core), vir: 16 (over z, x).
Axes of the slice: x: 4, y: 4, z: 4, core: 2. Of those that a mesh axis runs over, the one named last changes fastest.
Arguments:
- amplitudes: bfloat16 [9216, 16384], P('occ', 'vir'), may hold values from -6 to 6
- integrals: bfloat16 [16, 8, 1024, 1024], P('vir'), may hold values from -0.0625 to 0.0625
- cd_tiles: int32 [16, 8], P('vir'), may hold values from 0 to 15, as said below
- cd_count: int32 [16], P('vir'), may hold values from 1 to 8, as said below
Outputs:
- residual: bfloat16 [9216, 16384], P('occ', 'vir')
Inputs may be any that keep to these rules, and one draw needn't show every extreme that they name: `cd_tiles`: entries of one row are distinct and the first is the row's own pair tile. `cd_count`: slots at or past the count are unused.
All inputs are finite; a program needn't handle non-finite values.
Results may differ from a plain program's by a relative error of at most 0.0075.
Values may be sent and summed in bfloat16 or wider, within the bound.
No kernel may reach another device: no remote copies, remote signals or barrier semaphores. Data moves between devices by JAX's collectives and lax.ppermute only.
A program may use at most 128 MiB of HBM per device.

v0:
```python
import jax
import jax.numpy as jnp
from jax import lax
from jax.sharding import PartitionSpec as P

TW = 32
K = 1024
OCC_DEV = 12
CD_MAX = 8


def swapped(shard, axis, apart):
    return lax.ppermute(shard, axis, [(i, i ^ 1 << apart) for i in range(lax.axis_size(axis))])


def reflect_rows(matrix):
    occ_devices = lax.axis_size("occ")
    reshaped = matrix.reshape(OCC_DEV, occ_devices, OCC_DEV, matrix.shape[1])
    arrived = lax.all_to_all(reshaped, "occ", split_axis=1, concat_axis=1, tiled=True)
    return arrived.transpose(2, 1, 0, 3).reshape(matrix.shape)


def reflect_tiles(matrix):
    arrived = swapped(matrix, "vir", 0)
    row_count = matrix.shape[0]
    return arrived.reshape(row_count, TW, TW).transpose(0, 2, 1).reshape(row_count, K)


def on_device(amplitudes, integrals, cd_tiles, cd_count):
    row_count = amplitudes.shape[0]
    listed = cd_tiles[0]
    live_count = cd_count[0]
    blocks = integrals[0]
    zero_block = jnp.zeros((row_count, K), jnp.float32)

    def product(col_tile, slot_index):
        int_block = lax.dynamic_index_in_dim(blocks, slot_index, 0, keepdims=False)
        return lax.dot_general(
            col_tile, int_block, (((1,), (1,)), ((), ())), preferred_element_type=jnp.float32
        )

    gathered = lax.all_gather(amplitudes, "vir", axis=1, tiled=True)

    def visit_slot(slot_pos, running):
        tile_id = listed[slot_pos]

        def apply_block(current):
            col_tile = lax.dynamic_slice_in_dim(gathered, tile_id * K, K, 1)
            return current + product(col_tile, slot_pos)

        return lax.cond(slot_pos < live_count, apply_block, lambda current: current, running)

    ladder = lax.fori_loop(0, CD_MAX, visit_slot, zero_block)
    ladder = ladder.astype(jnp.bfloat16)
    mirrored = reflect_tiles(reflect_rows(ladder))
    summed = ladder.astype(jnp.float32) + mirrored.astype(jnp.float32)
    return summed.astype(jnp.bfloat16)


def solution(mesh):
    placed = (P("occ", "vir"), P("vir", None, None, None), P("vir", None), P("vir"))
    return jax.shard_map(
        on_device, mesh=mesh, in_specs=placed, out_specs=P("occ", "vir"), check_vma=False
    )
```

profile of v0, /device:TPU:6, one launch (start us, length us, event | category | flops | bytes accessed | tf_op | source)
XLA Modules:
  0.0 456.2 jit_solution(4664653060656685572)
XLA Ops:
  7.3 223.1 %all-gather.2.cloned.1.call-done = bf16[1152,16384]{1,0:T(8,128)(2,1)} async-done(((bf16[1152,1024]{1,0:T(8,128)(2,1)}), bf16[1152,16384]{1,0:T(8,128)(2,1)}) %all-gather.2.cloned.1.call-update) | async-done | bytes 37748752 | tf_op jit(solution)/shard_map/all_gather | solution.py:42
  233.1 83.6 %while.16 = (s32[]{:T(128)}, f32[1152,1024]{1,0:T(8,128)}, s32[]{:T(128)}, s32[8]{0:T(128)S(1)}, bf16[1152,16384]{1,0:T(8,128)(2,1)}, /*index=5*/bf16[8,1024,1024]{2,1,0:T(8,128)(2,1)}, s32[]{:T(128)}) while((s32[]{:T(128)}, f32[1152,1024]{1,0:T(8,128)}, s32[]{:T(128)}, s32[8]{0:T(128)S(1)}, bf16[1152,16384]{1,0:T(8,128)(2,1)}, ...), condition=%wide.region_3.4_spmd, body=%wide.region_0.3_spmd.sunk | while | flops 2417098752 | bytes 13893871 | solution.py:53
  233.8 9.8 %conditional.2 = (f32[1152,1024]{1,0:T(8,128)}) conditional(s32[]{:T(128)} %convert_element_type.41, f32[1152,1024]{1,0:T(8,128)} %get-tuple-element.236, (s32[]{:T(128)}, s32[8]{0:T(128)S(1)}, bf16[1152,16384]{1,0:T(8,128)(2,1)}, bf16[8,1024,1024]{2,1,0:T(8,128)(2,1)}, f32[1152,1024]{1,0:T(8,128)}) %tuple.45), branch_computations={%region_1.0_spmd, %region_2.2_spmd} | conditional | flops 2417098752 | bytes 13893740 | solution.py:51
  235.1 8.5 %convolution_add_fusion = f32[1152,1024]{1,0:T(8,128)} fusion(f32[1152,1024]{1,0:T(8,128)} %get-tuple-element.165, bf16[1152,16384]{1,0:T(8,128)(2,1)} %get-tuple-element.166, s32[]{:T(128)S(6)} %select_n.19, bf16[8,1024,1024]{2,1,0:T(8,128)(2,1)} %get-tuple-element.169, s32[]{:T(128)S(6)} %select_n.18), kind=kOutput, calls=%fused_computation | convolution fusion | flops 2417098752 | bytes 13893640 | tf_op jit(solution)/shard_map/while/body/eval_jaxpr/cond/branch_1_fun/dot_general | solution.py:38
  244.2 9.8 %conditional.2 = (f32[1152,1024]{1,0:T(8,128)}) conditional(s32[]{:T(128)} %convert_element_type.41, f32[1152,1024]{1,0:T(8,128)} %get-tuple-element.236, (s32[]{:T(128)}, s32[8]{0:T(128)S(1)}, bf16[1152,16384]{1,0:T(8,128)(2,1)}, bf16[8,1024,1024]{2,1,0:T(8,128)(2,1)}, f32[1152,1024]{1,0:T(8,128)}) %tuple.45), branch_computations={%region_1.0_spmd, %region_2.2_spmd} | conditional | flops 2417098752 | bytes 13893740 | solution.py:51
  245.5 8.5 %convolution_add_fusion = f32[1152,1024]{1,0:T(8,128)} fusion(f32[1152,1024]{1,0:T(8,128)} %get-tuple-element.165, bf16[1152,16384]{1,0:T(8,128)(2,1)} %get-tuple-element.166, s32[]{:T(128)S(6)} %select_n.19, bf16[8,1024,1024]{2,1,0:T(8,128)(2,1)} %get-tuple-element.169, s32[]{:T(128)S(6)} %select_n.18), kind=kOutput, calls=%fused_computation | convolution fusion | flops 2417098752 | bytes 13893640 | tf_op jit(solution)/shard_map/while/body/eval_jaxpr/cond/branch_1_fun/dot_general | solution.py:38
  254.7 9.8 %conditional.2 = (f32[1152,1024]{1,0:T(8,128)}) conditional(s32[]{:T(128)} %convert_element_type.41, f32[1152,1024]{1,0:T(8,128)} %get-tuple-element.236, (s32[]{:T(128)}, s32[8]{0:T(128)S(1)}, bf16[1152,16384]{1,0:T(8,128)(2,1)}, bf16[8,1024,1024]{2,1,0:T(8,128)(2,1)}, f32[1152,1024]{1,0:T(8,128)}) %tuple.45), branch_computations={%region_1.0_spmd, %region_2.2_spmd} | conditional | flops 2417098752 | bytes 13893740 | solution.py:51
  256.0 8.5 %convolution_add_fusion = f32[1152,1024]{1,0:T(8,128)} fusion(f32[1152,1024]{1,0:T(8,128)} %get-tuple-element.165, bf16[1152,16384]{1,0:T(8,128)(2,1)} %get-tuple-element.166, s32[]{:T(128)S(6)} %select_n.19, bf16[8,1024,1024]{2,1,0:T(8,128)(2,1)} %get-tuple-element.169, s32[]{:T(128)S(6)} %select_n.18), kind=kOutput, calls=%fused_computation | convolution fusion | flops 2417098752 | bytes 13893640 | tf_op jit(solution)/shard_map/while/body/eval_jaxpr/cond/branch_1_fun/dot_general | solution.py:38
  265.1 9.8 %conditional.2 = (f32[1152,1024]{1,0:T(8,128)}) conditional(s32[]{:T(128)} %convert_element_type.41, f32[1152,1024]{1,0:T(8,128)} %get-tuple-element.236, (s32[]{:T(128)}, s32[8]{0:T(128)S(1)}, bf16[1152,16384]{1,0:T(8,128)(2,1)}, bf16[8,1024,1024]{2,1,0:T(8,128)(2,1)}, f32[1152,1024]{1,0:T(8,128)}) %tuple.45), branch_computations={%region_1.0_spmd, %region_2.2_spmd} | conditional | flops 2417098752 | bytes 13893740 | solution.py:51
  266.4 8.5 %convolution_add_fusion = f32[1152,1024]{1,0:T(8,128)} fusion(f32[1152,1024]{1,0:T(8,128)} %get-tuple-element.165, bf16[1152,16384]{1,0:T(8,128)(2,1)} %get-tuple-element.166, s32[]{:T(128)S(6)} %select_n.19, bf16[8,1024,1024]{2,1,0:T(8,128)(2,1)} %get-tuple-element.169, s32[]{:T(128)S(6)} %select_n.18), kind=kOutput, calls=%fused_computation | convolution fusion | flops 2417098752 | bytes 13893640 | tf_op jit(solution)/shard_map/while/body/eval_jaxpr/cond/branch_1_fun/dot_general | solution.py:38
  275.6 9.8 %conditional.2 = (f32[1152,1024]{1,0:T(8,128)}) conditional(s32[]{:T(128)} %convert_element_type.41, f32[1152,1024]{1,0:T(8,128)} %get-tuple-element.236, (s32[]{:T(128)}, s32[8]{0:T(128)S(1)}, bf16[1152,16384]{1,0:T(8,128)(2,1)}, bf16[8,1024,1024]{2,1,0:T(8,128)(2,1)}, f32[1152,1024]{1,0:T(8,128)}) %tuple.45), branch_computations={%region_1.0_spmd, %region_2.2_spmd} | conditional | flops 2417098752 | bytes 13893740 | solution.py:51
  276.8 8.5 %convolution_add_fusion = f32[1152,1024]{1,0:T(8,128)} fusion(f32[1152,1024]{1,0:T(8,128)} %get-tuple-element.165, bf16[1152,16384]{1,0:T(8,128)(2,1)} %get-tuple-element.166, s32[]{:T(128)S(6)} %select_n.19, bf16[8,1024,1024]{2,1,0:T(8,128)(2,1)} %get-tuple-element.169, s32[]{:T(128)S(6)} %select_n.18), kind=kOutput, calls=%fused_computation | convolution fusion | flops 2417098752 | bytes 13893640 | tf_op jit(solution)/shard_map/while/body/eval_jaxpr/cond/branch_1_fun/dot_general | solution.py:38
  286.0 9.8 %conditional.2 = (f32[1152,1024]{1,0:T(8,128)}) conditional(s32[]{:T(128)} %convert_element_type.41, f32[1152,1024]{1,0:T(8,128)} %get-tuple-element.236, (s32[]{:T(128)}, s32[8]{0:T(128)S(1)}, bf16[1152,16384]{1,0:T(8,128)(2,1)}, bf16[8,1024,1024]{2,1,0:T(8,128)(2,1)}, f32[1152,1024]{1,0:T(8,128)}) %tuple.45), branch_computations={%region_1.0_spmd, %region_2.2_spmd} | conditional | flops 2417098752 | bytes 13893740 | solution.py:51
  287.3 8.5 %convolution_add_fusion = f32[1152,1024]{1,0:T(8,128)} fusion(f32[1152,1024]{1,0:T(8,128)} %get-tuple-element.165, bf16[1152,16384]{1,0:T(8,128)(2,1)} %get-tuple-element.166, s32[]{:T(128)S(6)} %select_n.19, bf16[8,1024,1024]{2,1,0:T(8,128)(2,1)} %get-tuple-element.169, s32[]{:T(128)S(6)} %select_n.18), kind=kOutput, calls=%fused_computation | convolution fusion | flops 2417098752 | bytes 13893640 | tf_op jit(solution)/shard_map/while/body/eval_jaxpr/cond/branch_1_fun/dot_general | solution.py:38
  296.5 9.8 %conditional.2 = (f32[1152,1024]{1,0:T(8,128)}) conditional(s32[]{:T(128)} %convert_element_type.41, f32[1152,1024]{1,0:T(8,128)} %get-tuple-element.236, (s32[]{:T(128)}, s32[8]{0:T(128)S(1)}, bf16[1152,16384]{1,0:T(8,128)(2,1)}, bf16[8,1024,1024]{2,1,0:T(8,128)(2,1)}, f32[1152,1024]{1,0:T(8,128)}) %tuple.45), branch_computations={%region_1.0_spmd, %region_2.2_spmd} | conditional | flops 2417098752 | bytes 13893740 | solution.py:51
  297.7 8.5 %convolution_add_fusion = f32[1152,1024]{1,0:T(8,128)} fusion(f32[1152,1024]{1,0:T(8,128)} %get-tuple-element.165, bf16[1152,16384]{1,0:T(8,128)(2,1)} %get-tuple-element.166, s32[]{:T(128)S(6)} %select_n.19, bf16[8,1024,1024]{2,1,0:T(8,128)(2,1)} %get-tuple-element.169, s32[]{:T(128)S(6)} %select_n.18), kind=kOutput, calls=%fused_computation | convolution fusion | flops 2417098752 | bytes 13893640 | tf_op jit(solution)/shard_map/while/body/eval_jaxpr/cond/branch_1_fun/dot_general | solution.py:38
  306.9 9.8 %conditional.2 = (f32[1152,1024]{1,0:T(8,128)}) conditional(s32[]{:T(128)} %convert_element_type.41, f32[1152,1024]{1,0:T(8,128)} %get-tuple-element.236, (s32[]{:T(128)}, s32[8]{0:T(128)S(1)}, bf16[1152,16384]{1,0:T(8,128)(2,1)}, bf16[8,1024,1024]{2,1,0:T(8,128)(2,1)}, f32[1152,1024]{1,0:T(8,128)}) %tuple.45), branch_computations={%region_1.0_spmd, %region_2.2_spmd} | conditional | flops 2417098752 | bytes 13893740 | solution.py:51
  308.2 8.5 %convolution_add_fusion = f32[1152,1024]{1,0:T(8,128)} fusion(f32[1152,1024]{1,0:T(8,128)} %get-tuple-element.165, bf16[1152,16384]{1,0:T(8,128)(2,1)} %get-tuple-element.166, s32[]{:T(128)S(6)} %select_n.19, bf16[8,1024,1024]{2,1,0:T(8,128)(2,1)} %get-tuple-element.169, s32[]{:T(128)S(6)} %select_n.18), kind=kOutput, calls=%fused_computation | convolution fusion | flops 2417098752 | bytes 13893640 | tf_op jit(solution)/shard_map/while/body/eval_jaxpr/cond/branch_1_fun/dot_general | solution.py:38
  322.8 4.8 %reshape.14 = bf16[12,8,12,1024]{3,2,1,0:T(8,128)(2,1)} reshape(bf16[1152,1024]{1,0:T(8,128)(2,1)} %copy.12) | data formatting | bytes 4718592 | tf_op jit(solution)/shard_map/reshape | solution.py:18
  330.1 42.5 %all_to_all.5 = bf16[12,8,12,1024]{3,2,0,1:T(8,128)(2,1)S(1)} all-to-all(bf16[12,8,12,1024]{3,2,0,1:T(8,128)(2,1)S(1)} %copy.13), channel_id=1, replica_groups=mesh['occ'=8,'vir'=16] {'occ'}, dimensions={1} | all-to-all | bytes 4718592 | tf_op jit(solution)/shard_map/all_to_all | solution.py:19
  375.6 4.9 %reshape.15 = bf16[1152,1024]{1,0:T(8,128)(2,1)} reshape(bf16[12,8,12,1024]{3,2,1,0:T(8,128)(2,1)} %copy.14) | data formatting | bytes 4718592 | tf_op jit(solution)/shard_map/reshape | solution.py:20
  380.5 52.9 %collective-permute-done = bf16[1152,1024]{1,0:T(8,128)(2,1)} collective-permute-done((bf16[1152,1024]{1,0:T(8,128)(2,1)}, bf16[1152,1024]{1,0:T(8,128)(2,1)}, u32[]{:S(2)}, u32[]{:S(2)}) %collective-permute-start) | collective-permute-done | bytes 2359328 | tf_op jit(solution)/shard_map/ppermute | solution.py:13
  433.4 4.6 copy.15
  438.0 5.1 %copy.16 = f32[1152,32,32]{0,2,1:T(8,128)S(1)} copy(f32[1152,32,32]{0,1,2:T(8,128)} %bitcast.15) | data formatting | bytes 9437184 | tf_op jit(solution)/shard_map/convert_element_type | solution.py:56
  (20 shorter events, 26.1 us)
Async XLA Ops:
  6.5 226.6 %copy-start = (s32[1,8]{1,0:T(1,128)S(1)}, s32[1,8]{1,0:T(1,128)}, u32[]{:S(2)}) copy-start(s32[1,8]{1,0:T(1,128)} %param.10) | copy-start | bytes 100
  6.5 223.8 %all-gather.2.cloned.1.call-start = ((), (), s32[]{:S(2)}) async-start(), calls=%async_computation.1 | async-start | bytes 40108032 | tf_op jit(solution)/shard_map/all_gather | solution.py:42
  380.5 52.9 %collective-permute-start = (bf16[1152,1024]{1,0:T(8,128)(2,1)}, bf16[1152,1024]{1,0:T(8,128)(2,1)}, u32[]{:S(2)}, u32[]{:S(2)}) collective-permute-start(bf16[1152,1024]{1,0:T(8,128)(2,1)} %reshape.15), channel_id=1, source_target_pairs={{0,1},{1,0},{2,3},{3,2},{4,5},{5,4},{6,7},{7,6},{8,9},{9,8},{10,11... | collective-permute-start | bytes 7077896 | tf_op jit(solution)/shard_map/ppermute | solution.py:13
Sparse Core Ops, SparseCore 0:
  9.5 220.8 all-gather.1
where the time goes:
time: 457 us; the launch traced here: 456 us
  waiting for transfers between devices  277 us (61%)
  matrix products  68.2 us (15%)
  local copies, waits for them, and re-layouts  42.8 us (9%)
  blocking collectives  42.5 us (9%)
  between operations  13.4 us (3%)
  loops' own time  10.5 us (2%)
    all_gather x1, waiting for transfers between devices, on_device(): gathered = lax.all_gather(amplitudes, 'vir', axis=1, tiled=True)  223 us
    dot_general x8, matrix products, product(): lax.dot_general(col_tile, int_block, (((1,), (1,)), ((), ())), preferred_...  68.2 us
    ppermute x1, waiting for transfers between devices, swapped(): lax.ppermute(shard, axis, [(i, i ^ 1 << apart) for i in range(lax.axis_si...  52.9 us
    all_to_all x1, blocking collectives, reflect_rows(): lax.all_to_all(reshaped, 'occ', split_axis=1, concat_axis=1, tiled=True)  42.5 us
    convert_element_type x2, local copies, waits for them, and re-layouts, on_device(): summed = ladder.astype(jnp.float32) + mirrored.astype(jnp.float32)  9.62 us
  transfers between devices with their start and end apart: 2, of which 2 were waited for; matrix products, arithmetic and copies ran while one was open for 0% of the time, Pallas kernels for 0%

commit v1 on v0

--- a/solution.py
+++ b/solution.py
@@ -39,7 +39,8 @@
             col_tile, int_block, (((1,), (1,)), ((), ())), preferred_element_type=jnp.float32
         )
 
-    gathered = lax.all_gather(amplitudes, "vir", axis=1, tiled=True)
+    sent = jnp.stack([amplitudes] * lax.axis_size("vir"))
+    gathered = jnp.concatenate(lax.all_to_all(sent, "vir", 0, 0), axis=1)
 
     def visit_slot(slot_pos, running):
         tile_id = listed[slot_pos]

time: 457 us -> 895 us (1.96)
  waiting for transfers between devices: 277 us -> 608 us
  local copies, waits for them, and re-layouts: 42.8 us -> 148 us
  between operations: 13.4 us -> 0.03 us
    all_to_all x0 -> x1, waiting for transfers between devices: none -> 555 us  [on_device(): gathered = jnp.concatenate(lax.all_to_all(sent, 'vir', 0, 0), axis=1)]
    all_gather x1 -> x0, waiting for transfers between devices: 223 us -> none  [on_device(): gathered = lax.all_gather(amplitudes, 'vir', axis=1, tiled=True)]
    while x1 -> x2, local copies, waits for them, and re-layouts: 3.58 us -> 51.3 us  [on_device(): ladder = lax.fori_loop(0, CD_MAX, visit_slot, zero_block)]
    all_to_all x0 -> x1, local copies, waits for them, and re-layouts: none -> 43.7 us  [on_device(): gathered = jnp.concatenate(lax.all_to_all(sent, 'vir', 0, 0), axis=1)]
    another operation x0 -> x1, local copies, waits for them, and re-layouts: none -> 13.6 us  [on_device(): sent = jnp.stack([amplitudes] * lax.axis_size('vir'))]
where the time goes in v1:
time: 895 us; the launch traced here: 888 us
  waiting for transfers between devices  608 us (68%)
  local copies, waits for them, and re-layouts  148 us (17%)
  matrix products  68 us (8%)
  blocking collectives  42.7 us (5%)
  loops' own time  10.5 us (1%)
    all_to_all x1, waiting for transfers between devices, on_device(): gathered = jnp.concatenate(lax.all_to_all(sent, 'vir', 0, 0), axis=1)  555 us
    dot_general x8, matrix products, product(): lax.dot_general(col_tile, int_block, (((1,), (1,)), ((), ())), preferred_...  68 us
    ppermute x1, waiting for transfers between devices, swapped(): lax.ppermute(shard, axis, [(i, i ^ 1 << apart) for i in range(lax.axis_si...  52.9 us
    while x2, local copies, waits for them, and re-layouts, on_device(): ladder = lax.fori_loop(0, CD_MAX, visit_slot, zero_block)  51.3 us
    all_to_all x1, local copies, waits for them, and re-layouts, on_device(): gathered = jnp.concatenate(lax.all_to_all(sent, 'vir', 0, 0), axis=1)  43.7 us
    all_to_all x1, blocking collectives, reflect_rows(): lax.all_to_all(reshaped, 'occ', split_axis=1, concat_axis=1, tiled=True)  42.7 us
  transfers between devices with their start and end apart: 2, of which 2 were waited for; matrix products, arithmetic and copies ran while one was open for 0% of the time, Pallas kernels for 0%

profile of v1, /device:TPU:6, one launch (start us, length us, event | category | flops | bytes accessed | tf_op | source)
XLA Modules:
  0.0 887.9 jit_solution(4209219337471703904)
XLA Ops:
  0.0 13.6 %stack.2 = bf16[16,1152,1024]{2,1,0:T(8,128)(2,1)} broadcast(bf16[1152,1024]{1,0:T(8,128)(2,1)} %param.8), dimensions={1,2} | broadcast | bytes 40108032 | tf_op jit(solution)/shard_map/stack | solution.py:42
  13.6 8.3 all-to-all-start
  21.9 555.4 %all-to-all-done = bf16[16,1152,1024]{2,1,0:T(8,128)(2,1)} async-done(((bf16[16,1152,1024]{2,1,0:T(8,128)(2,1)}), bf16[16,1152,1024]{2,1,0:T(8,128)(2,1)}, u32[]{:S(2)}, u32[]{:S(2)}) %all-to-all-start) | async-done | bytes 37748768 | tf_op jit(solution)/shard_map/all_to_all | solution.py:43
  577.3 43.7 %copy.18 = bf16[16,1152,1024]{1,2,0:T(8,128)(2,1)} copy(bf16[16,1152,1024]{2,1,0:T(8,128)(2,1)} %all-to-all-done) | data formatting | bytes 75497472 | tf_op jit(solution)/shard_map/all_to_all | solution.py:43
  620.9 47.7 %copy.19 = bf16[1152,16384]{1,0:T(8,128)(2,1)} copy(bf16[1152,16384]{0,1:T(8,128)(2,1)} %bitcast.18) | data formatting | bytes 75497472 | tf_op jit(solution)/shard_map/while | solution.py:54
  671.4 83.7 %while.16 = (s32[]{:T(128)}, f32[1152,1024]{1,0:T(8,128)}, s32[]{:T(128)}, s32[8]{0:T(128)S(1)}, bf16[1152,16384]{1,0:T(8,128)(2,1)}, /*index=5*/bf16[8,1024,1024]{2,1,0:T(8,128)(2,1)}, s32[]{:T(128)}) while((s32[]{:T(128)}, f32[1152,1024]{1,0:T(8,128)}, s32[]{:T(128)}, s32[8]{0:T(128)S(1)}, bf16[1152,16384]{1,0:T(8,128)(2,1)}, ...), condition=%wide.region_3.4_spmd, body=%wide.region_0.3_spmd.sunk | while | flops 2417098752 | bytes 13893871 | solution.py:54
  672.0 9.8 %conditional.2 = (f32[1152,1024]{1,0:T(8,128)}) conditional(s32[]{:T(128)} %convert_element_type.41, f32[1152,1024]{1,0:T(8,128)} %get-tuple-element.242, (s32[]{:T(128)}, s32[8]{0:T(128)S(1)}, bf16[1152,16384]{1,0:T(8,128)(2,1)}, bf16[8,1024,1024]{2,1,0:T(8,128)(2,1)}, f32[1152,1024]{1,0:T(8,128)}) %tuple.46), branch_computations={%region_1.0_spmd, %region_2.2_spmd} | conditional | flops 2417098752 | bytes 13893740 | solution.py:52
  673.3 8.5 convolution_add_fusion
  682.5 9.8 %conditional.2 = (f32[1152,1024]{1,0:T(8,128)}) conditional(s32[]{:T(128)} %convert_element_type.41, f32[1152,1024]{1,0:T(8,128)} %get-tuple-element.242, (s32[]{:T(128)}, s32[8]{0:T(128)S(1)}, bf16[1152,16384]{1,0:T(8,128)(2,1)}, bf16[8,1024,1024]{2,1,0:T(8,128)(2,1)}, f32[1152,1024]{1,0:T(8,128)}) %tuple.46), branch_computations={%region_1.0_spmd, %region_2.2_spmd} | conditional | flops 2417098752 | bytes 13893740 | solution.py:52
  683.8 8.5 convolution_add_fusion
  693.0 9.8 %conditional.2 = (f32[1152,1024]{1,0:T(8,128)}) conditional(s32[]{:T(128)} %convert_element_type.41, f32[1152,1024]{1,0:T(8,128)} %get-tuple-element.242, (s32[]{:T(128)}, s32[8]{0:T(128)S(1)}, bf16[1152,16384]{1,0:T(8,128)(2,1)}, bf16[8,1024,1024]{2,1,0:T(8,128)(2,1)}, f32[1152,1024]{1,0:T(8,128)}) %tuple.46), branch_computations={%region_1.0_spmd, %region_2.2_spmd} | conditional | flops 2417098752 | bytes 13893740 | solution.py:52
  694.2 8.5 convolution_add_fusion
  703.4 9.8 %conditional.2 = (f32[1152,1024]{1,0:T(8,128)}) conditional(s32[]{:T(128)} %convert_element_type.41, f32[1152,1024]{1,0:T(8,128)} %get-tuple-element.242, (s32[]{:T(128)}, s32[8]{0:T(128)S(1)}, bf16[1152,16384]{1,0:T(8,128)(2,1)}, bf16[8,1024,1024]{2,1,0:T(8,128)(2,1)}, f32[1152,1024]{1,0:T(8,128)}) %tuple.46), branch_computations={%region_1.0_spmd, %region_2.2_spmd} | conditional | flops 2417098752 | bytes 13893740 | solution.py:52
  704.7 8.5 convolution_add_fusion
  713.9 9.8 %conditional.2 = (f32[1152,1024]{1,0:T(8,128)}) conditional(s32[]{:T(128)} %convert_element_type.41, f32[1152,1024]{1,0:T(8,128)} %get-tuple-element.242, (s32[]{:T(128)}, s32[8]{0:T(128)S(1)}, bf16[1152,16384]{1,0:T(8,128)(2,1)}, bf16[8,1024,1024]{2,1,0:T(8,128)(2,1)}, f32[1152,1024]{1,0:T(8,128)}) %tuple.46), branch_computations={%region_1.0_spmd, %region_2.2_spmd} | conditional | flops 2417098752 | bytes 13893740 | solution.py:52
  715.2 8.5 convolution_add_fusion
  724.3 9.8 %conditional.2 = (f32[1152,1024]{1,0:T(8,128)}) conditional(s32[]{:T(128)} %convert_element_type.41, f32[1152,1024]{1,0:T(8,128)} %get-tuple-element.242, (s32[]{:T(128)}, s32[8]{0:T(128)S(1)}, bf16[1152,16384]{1,0:T(8,128)(2,1)}, bf16[8,1024,1024]{2,1,0:T(8,128)(2,1)}, f32[1152,1024]{1,0:T(8,128)}) %tuple.46), branch_computations={%region_1.0_spmd, %region_2.2_spmd} | conditional | flops 2417098752 | bytes 13893740 | solution.py:52
  725.6 8.5 convolution_add_fusion
  734.8 9.8 %conditional.2 = (f32[1152,1024]{1,0:T(8,128)}) conditional(s32[]{:T(128)} %convert_element_type.41, f32[1152,1024]{1,0:T(8,128)} %get-tuple-element.242, (s32[]{:T(128)}, s32[8]{0:T(128)S(1)}, bf16[1152,16384]{1,0:T(8,128)(2,1)}, bf16[8,1024,1024]{2,1,0:T(8,128)(2,1)}, f32[1152,1024]{1,0:T(8,128)}) %tuple.46), branch_computations={%region_1.0_spmd, %region_2.2_spmd} | conditional | flops 2417098752 | bytes 13893740 | solution.py:52
  736.1 8.5 convolution_add_fusion
  745.2 9.8 %conditional.2 = (f32[1152,1024]{1,0:T(8,128)}) conditional(s32[]{:T(128)} %convert_element_type.41, f32[1152,1024]{1,0:T(8,128)} %get-tuple-element.242, (s32[]{:T(128)}, s32[8]{0:T(128)S(1)}, bf16[1152,16384]{1,0:T(8,128)(2,1)}, bf16[8,1024,1024]{2,1,0:T(8,128)(2,1)}, f32[1152,1024]{1,0:T(8,128)}) %tuple.46), branch_computations={%region_1.0_spmd, %region_2.2_spmd} | conditional | flops 2417098752 | bytes 13893740 | solution.py:52
  746.5 8.5 convolution_add_fusion
  768.4 42.7 %all_to_all.10 = bf16[12,8,12,1024]{3,2,0,1:T(8,128)(2,1)S(1)} all-to-all(bf16[12,8,12,1024]{3,2,0,1:T(8,128)(2,1)S(1)} %copy.22), channel_id=1, replica_groups=mesh['occ'=8,'vir'=16] {'occ'}, dimensions={1} | all-to-all | bytes 4718592 | tf_op jit(solution)/shard_map/all_to_all | solution.py:19
  819.1 52.9 %collective-permute-done = bf16[1152,1024]{1,0:T(8,128)(2,1)} collective-permute-done((bf16[1152,1024]{1,0:T(8,128)(2,1)}, bf16[1152,1024]{1,0:T(8,128)(2,1)}, u32[]{:S(2)}, u32[]{:S(2)}) %collective-permute-start) | collective-permute-done | bytes 2359328 | tf_op jit(solution)/shard_map/ppermute | solution.py:13
  (22 shorter events, 45.0 us)
Async XLA Ops:
  13.6 563.7 %all-to-all-start = ((bf16[16,1152,1024]{2,1,0:T(8,128)(2,1)}), bf16[16,1152,1024]{2,1,0:T(8,128)(2,1)}, u32[]{:S(2)}, u32[]{:S(2)}) async-start(bf16[16,1152,1024]{2,1,0:T(8,128)(2,1)} %stack.2), calls=%async_computation | async-start | bytes 75497472 | tf_op jit(solution)/shard_map/all_to_all | solution.py:43
  668.6 2.7 copy-start
  819.1 52.9 %collective-permute-start = (bf16[1152,1024]{1,0:T(8,128)(2,1)}, bf16[1152,1024]{1,0:T(8,128)(2,1)}, u32[]{:S(2)}, u32[]{:S(2)}) collective-permute-start(bf16[1152,1024]{1,0:T(8,128)(2,1)} %reshape.25), channel_id=1, source_target_pairs={{0,1},{1,0},{2,3},{3,2},{4,5},{5,4},{6,7},{7,6},{8,9},{9,8},{10,11... | collective-permute-start | bytes 7077896 | tf_op jit(solution)/shard_map/ppermute | solution.py:13
